TPU v7x, 256 devices: a whole 4x4x8 slice. The times are simulated.
256 devices in a mesh: dp: 32 (over x, y, core), ctx: 8 (over z).
Axes of the slice: x: 4, y: 4, z: 8, core: 2. Of those that a mesh axis runs over, the one named last changes fastest.
Arguments:
- cotangent: bfloat16 [32, 4096, 8192], P('dp', 'ctx'), may hold values from -6 to 6
- out_weight: bfloat16 [256, 8192], P(None, 'ctx'), may hold values from -0.0625 to 0.0625
- head_input: bfloat16 [32, 4096, 256], P('dp', 'ctx'), may hold values from -6 to 6
- injector: bfloat16 [32, 4096, 128], P('dp', 'ctx'), may hold values from -0.59765625 to 0.59765625
- readout: bfloat16 [32, 4096, 128], P('dp', 'ctx'), may hold values from -0.59765625 to 0.59765625
- decay_code: int32 [32, 4096, 2], P('dp', 'ctx'), may hold values from 1 to 40960
- decay_rate: float32 [2], replicated, may hold values from 4.8828125e-06 to 0.0061035156
- start_state: float32 [32, 8, 2, 128, 128], P('dp', 'ctx'), may hold values from -6 to 6
Outputs:
- gradient_input: bfloat16 [32, 4096, 256], P('dp', 'ctx')
- gradient_injector: float32 [32, 4096, 128], P('dp', 'ctx')
- gradient_readout: float32 [32, 4096, 128], P('dp', 'ctx')
- gradient_weight: float32 [256, 8192], P('ctx', 'dp')
- gradient_rate: float32 [2], replicated
All inputs are finite; a program needn't handle non-finite values.
Results may differ from a plain program's by a relative error of at most 0.0049.
Values may be sent and summed in bfloat16 or wider, within the bound.
No kernel may reach another device: no remote copies, remote signals or barrier semaphores. Data moves between devices by JAX's collectives and lax.ppermute only.
A program may use at most 128 MiB of HBM per device.

v0:
```python
import jax
import jax.numpy as jnp
from jax import lax
from jax.sharding import PartitionSpec as P

precise = lax.Precision.HIGHEST


def carried_in(value, axis, join, neutral):
    count, mine = (lax.axis_size(axis), lax.axis_index(axis))
    pieces = jax.tree.map(lambda part: lax.all_gather(part, axis), value)
    pieces = jax.tree.map(lambda part: part[::-1], pieces)
    mine = count - 1 - mine
    total = jax.tree.map(
        lambda part, zero: jnp.full_like(part, 0) + jnp.asarray(zero, part.dtype), value, neutral
    )

    def lap(position, total):
        longer = join(total, jax.tree.map(lambda part: part[position], pieces))
        return jax.tree.map(lambda new, old: jnp.where(position < mine, new, old), longer, total)

    return lax.fori_loop(0, count - 1, lap, total)


def decay_table(log_decay):
    cumulative = jnp.cumsum(log_decay, axis=0)
    length = log_decay.shape[0]
    row_index = lax.broadcasted_iota(jnp.int32, (length, length), 0)
    col_index = lax.broadcasted_iota(jnp.int32, (length, length), 1)
    causal = (row_index >= col_index)[None]
    spread = cumulative.T[:, :, None] - cumulative.T[:, None, :]
    weights = jnp.where(causal, jnp.exp(jnp.where(causal, spread, 0.0)), 0.0)
    return (cumulative, weights)


def forward_shard(head_input, injector, readout, log_decay, start_state):
    length, heads_count = log_decay.shape
    cumulative, weights = decay_table(log_decay)
    intersection = jnp.dot(readout, injector.T, preferred_element_type=jnp.float32)
    mixing = intersection[None] * weights
    inputs_heads = head_input.reshape(length, heads_count, -1).astype(jnp.float32)
    within = jnp.einsum("hts,shp->thp", mixing, inputs_heads, precision=precise)
    carried = jnp.einsum("tn,hpn->thp", readout.astype(jnp.float32), start_state, precision=precise)
    outputs = within + jnp.exp(cumulative)[:, :, None] * carried
    return outputs.reshape(length, -1).astype(jnp.bfloat16)


def chain_piece(readout, output_grad, log_decay):
    length, heads_count = log_decay.shape
    cumulative = jnp.cumsum(log_decay, axis=0)
    grad_heads = output_grad.reshape(length, heads_count, -1).astype(jnp.float32)
    scaled = jnp.exp(cumulative)[:, :, None] * readout.astype(jnp.float32)[:, None, :]
    adjoint = jnp.einsum("thp,thn->hpn", grad_heads, scaled, precision=precise)
    return (jnp.exp(cumulative[-1]), adjoint)


def backward_shard(head_input, injector, readout, output_grad, log_decay, start_state, incoming):
    length, heads_count = log_decay.shape
    cumulative, weights = decay_table(log_decay)
    inputs_narrow = head_input.reshape(length, heads_count, -1)
    grad_narrow = output_grad.reshape(length, heads_count, -1)
    inputs_heads = inputs_narrow.astype(jnp.float32)
    grad_heads = grad_narrow.astype(jnp.float32)
    inject_float = injector.astype(jnp.float32)
    read_float = readout.astype(jnp.float32)
    intersection = jnp.dot(readout, injector.T, preferred_element_type=jnp.float32)
    mixing = intersection[None] * weights
    to_end = jnp.exp(cumulative[-1][None, :] - cumulative)
    from_start = jnp.exp(cumulative)
    entering = jnp.einsum("sn,hpn->shp", inject_float, incoming, precision=precise)
    grad_input = (
        jnp.einsum("hts,thp->shp", mixing, grad_heads, precision=precise)
        + to_end[:, :, None] * entering
    )
    pairing = (
        jnp.einsum("thp,shp->hts", grad_narrow, inputs_narrow, preferred_element_type=jnp.float32)
        * weights
    )
    through_start = jnp.einsum("thp,hpn->thn", grad_heads, start_state, precision=precise)
    grad_read = jnp.einsum("hts,sn->tn", pairing, inject_float, precision=precise)
    grad_read = grad_read + jnp.einsum("th,thn->tn", from_start, through_start, precision=precise)
    input_state = jnp.einsum("shp,hpn->shn", inputs_heads, incoming, precision=precise)
    grad_inject = jnp.einsum("hts,tn->sn", pairing, read_float, precision=precise)
    grad_inject = grad_inject + jnp.einsum("sh,shn->sn", to_end, input_state, precision=precise)
    products = intersection[None] * pairing
    carried = (
        jnp.einsum("tn,hpn->thp", read_float, start_state, precision=precise)
        * from_start[:, :, None]
    )
    reaching = to_end * jnp.einsum("shn,sn->sh", input_state, inject_float, precision=precise)
    end_term = from_start[-1] * jnp.einsum(
        "hpn,hpn->h", incoming, start_state, precision=precise
    ) + jnp.sum(reaching, axis=0)
    cumul_grad = jnp.sum(products, axis=2).T - jnp.sum(products, axis=1).T
    cumul_grad = cumul_grad + jnp.sum(grad_heads * carried, axis=2) - reaching
    is_last = lax.broadcasted_iota(jnp.int32, (length, 1), 0) == length - 1
    cumul_grad = cumul_grad + jnp.where(is_last, end_term[None, :], 0.0)
    decay_grad = jnp.flip(jnp.cumsum(jnp.flip(cumul_grad, 0), axis=0), 0)
    rate_terms = jnp.sum(decay_grad * log_decay, axis=0)
    return (grad_input.reshape(length, -1).astype(jnp.bfloat16), grad_inject, grad_read, rate_terms)


def combine(earlier, later):
    return (later[0] * earlier[0], later[1] + later[0][:, None, None] * earlier[1])


def local(
    cotangent, out_weight, head_input, injector, readout, decay_code, decay_rate, start_state
):
    grad_out = cotangent[0]
    inputs_local = head_input[0]
    inject_local = injector[0]
    read_local = readout[0]
    state_local = start_state[0, 0]
    length = grad_out.shape[0]
    output_grad = lax.dot_general(
        grad_out,
        lax.all_gather(out_weight, "ctx", axis=1, tiled=True),
        (((1,), (1,)), ((), ())),
        preferred_element_type=jnp.float32,
    ).astype(jnp.bfloat16)
    log_decay = -decay_rate[None, :] * decay_code[0].astype(jnp.float32)
    decay_total, adjoint = chain_piece(read_local, output_grad, log_decay)
    identity = (jnp.ones_like(decay_total), jnp.zeros_like(adjoint))
    incoming = carried_in((decay_total, adjoint), "ctx", combine, identity)[1]
    outputs = forward_shard(inputs_local, inject_local, read_local, log_decay, state_local)
    local_weight = lax.dot_general(
        outputs, grad_out, (((0,), (0,)), ((), ())), preferred_element_type=jnp.float32
    )
    data_part = lax.psum_scatter(local_weight, "dp", scatter_dimension=1, tiled=True)
    weight_part = lax.psum_scatter(data_part, "ctx", scatter_dimension=0, tiled=True)
    grad_input, grad_inject, grad_read, rate_terms = backward_shard(
        inputs_local, inject_local, read_local, output_grad, log_decay, state_local, incoming
    )
    tokens_all = length * lax.axis_size("dp") * lax.axis_size("ctx")
    rate_sum = lax.psum(rate_terms, ("dp", "ctx"))
    return (
        grad_input[None],
        grad_inject[None],
        grad_read[None],
        weight_part,
        rate_sum / tokens_all,
    )


def solution(mesh):
    in_specs = (
        P("dp", "ctx", None),
        P(None, "ctx"),
        P("dp", "ctx", None),
        P("dp", "ctx", None),
        P("dp", "ctx", None),
        P("dp", "ctx", None),
        P(),
        P("dp", "ctx", None, None, None),
    )
    out_specs = (
        P("dp", "ctx", None),
        P("dp", "ctx", None),
        P("dp", "ctx", None),
        P("ctx", "dp"),
        P(),
    )
    return jax.shard_map(local, mesh=mesh, in_specs=in_specs, out_specs=out_specs, check_vma=False)
```

profile of v0, /device:TPU:2, one launch (start us, length us, event | category | flops | bytes accessed | tf_op | source)
XLA Modules:
  0.0 262.4 jit_solution(3269358175071123547)
XLA Ops:
  7.2 0.7 all-gather.5.cloned.1.call-update
  7.9 0.7 neg.4
  8.6 0.8 fusion.61
  9.4 0.6 reduce-window.14
  10.0 0.2 slice_reduce_fusion.1
  10.1 0.2 reduce-window.15
  10.3 0.9 bitcast_convert_fusion.1
  11.3 0.1 copy.52
  11.5 56.1 %all-gather.5.cloned.1.call-done = bf16[256,8192]{1,0:T(8,128)(2,1)} async-done(((bf16[256,1024]{1,0:T(8,128)(2,1)}), bf16[256,8192]{1,0:T(8,128)(2,1)}) %all-gather.5.cloned.1.call-update) | async-done | bytes 4194320 | tf_op jit(solution)/shard_map/all_gather | solution.py:118
  67.6 6.9 %fusion.26 = bf16[512,256]{0,1:T(8,128)(2,1)S(1)} fusion(bf16[256,8192]{1,0:T(8,128)(2,1)} %all-gather.5.cloned.1.call-done, bf16[1,512,8192]{2,1,0:T(8,128)(2,1)} %param.10), kind=kOutput, calls=%fused_computation.24 | convolution fusion | flops 2147614720 | bytes 12845056 | tf_op jit(solution)/shard_map/dot_general | solution.py:116
  74.6 1.1 fusion.43
  75.7 0.1 copy.91
  76.0 0.3 fusion.55
  76.3 0.4 multiply_reduce_fusion.2
  76.8 2.0 fusion.22
  78.7 9.1 %fusion.1 = f32[256,8192]{1,0:T(8,128)} fusion(bf16[512,256]{0,1:T(8,128)(2,1)S(1)} %bitcast.164, bf16[1,512,8192]{2,1,0:T(8,128)(2,1)} %param.10), kind=kOutput, calls=%fused_computation.3 | convolution fusion | flops 2147483648 | bytes 17039360 | tf_op jit(solution)/shard_map/dot_general | solution.py:127
  87.9 0.2 slice_reduce_fusion.3
  88.0 14.7 %all-gather.1 = f32[8,1,2]{2,1,0:T(1,128)S(1)} all-gather(f32[1,1,2]{2,1,0:T(1,128)S(1)} %bitcast.175), channel_id=1, replica_groups=mesh['dp'=32,'ctx'=8] {'ctx'}, dimensions={0}, use_global_device_ids=true | all-gather | bytes 72 | tf_op jit(solution)/shard_map/all_gather | solution.py:11
  102.9 0.1 rev.14
  103.0 0.1 copy.72
  103.2 0.1 copy.89
  103.4 0.2 slice_reduce_fusion.2
  103.6 0.4 convolution_bitcast_fusion
  104.0 4.4 %fusion.45 = f32[512,1,128]{2,1,0:T(1,128)} fusion(f32[512,2,1]{1,2,0:T(1,128)S(1)} %copy.72, f32[512,2,128]{2,0,1:T(8,128)S(1)} %convolution_bitcast_fusion), kind=kOutput, calls=%fused_computation.47 | convolution fusion | flops 1572864 | bytes 790528 | tf_op jit(solution)/shard_map/th,thn->tn/dot_general | solution.py:81
  108.4 2.4 fusion.11
  110.8 2.2 multiply_reduce_fusion
  113.0 0.1 all-gather.7.cloned.1.call-done
  113.1 1.3 rev.13
  114.5 0.9 while.14
  114.5 0.1 fusion.81
  115.4 0.1 fusion.49
  115.5 0.4 fusion.41
  115.9 0.2 multiply_reduce_fusion.4
  116.2 0.4 rev.15
  116.6 0.6 reduce-window.16
  117.2 0.2 slice_reduce_fusion
  117.4 0.2 reduce-window.19
  117.6 0.4 rev.16
  118.0 0.2 multiply_reduce_fusion.3
  118.2 1.3 fusion.29
  119.5 75.2 %psum.7 = f32[2]{0:T(128)S(1)} all-reduce(f32[2]{0:T(128)S(1)} %multiply_reduce_fusion.3), channel_id=1, replica_groups=mesh['dp'=32,'ctx'=8] {'dp','ctx'}, use_global_device_ids=true, to_apply=%region_14.15 | all-reduce | flops 2 | bytes 16 | tf_op jit(solution)/shard_map/psum | solution.py:136
  194.8 0.1 copy.70
  194.9 21.4 %reduce-scatter.3.cloned.1.call-done = f32[256,256]{1,0:T(8,128)} async-done(((f32[256,8192]{1,0:T(8,128)}), f32[256,256]{1,0:T(8,128)}) %reduce-scatter.3.cloned.1.call-update) | async-done | bytes 262160 | tf_op jit(solution)/shard_map/reduce_scatter | solution.py:130
  216.3 0.4 fusion.25
  216.7 0.8 copy.62
  217.6 1.7 fusion.30
  219.3 0.5 broadcast_multiply_fusion
  219.8 36.1 %reduce-scatter.5.cloned.1.call-done = f32[32,256]{1,0:T(8,128)} async-done(((f32[256,256]{1,0:T(8,128)}), f32[32,256]{1,0:T(8,128)}) %reduce-scatter.5.cloned.1.call-update) | async-done | bytes 32784 | tf_op jit(solution)/shard_map/reduce_scatter | solution.py:131
  (52 shorter events, 1.5 us)
Async XLA Ops:
  7.2 60.4 %all-gather.5.cloned.1.call-start = ((), (), s32[]{:S(2)}) async-start(), calls=%async_computation.2 | async-start | bytes 4718592 | tf_op jit(solution)/shard_map/all_gather | solution.py:118
  7.9 105.2 %all-gather.7.cloned.1.call-start = ((), (), s32[]{:S(2)}) async-start(), calls=%async_computation.5 | async-start | bytes 1179648 | tf_op jit(solution)/shard_map/all_gather | solution.py:11
  11.5 64.2 %copy-start.4 = (bf16[1,512,256]{2,1,0:T(8,128)(2,1)S(1)}, bf16[1,512,256]{2,1,0:T(8,128)(2,1)}, u32[]{:S(2)}) copy-start(bf16[1,512,256]{2,1,0:T(8,128)(2,1)} %param.12) | copy-start | bytes 786436
  11.5 64.5 %copy-start = (bf16[1,512,128]{2,1,0:T(8,128)(2,1)S(1)}, bf16[1,512,128]{2,1,0:T(8,128)(2,1)}, u32[]{:S(2)}) copy-start(bf16[1,512,128]{2,1,0:T(8,128)(2,1)} %param.13) | copy-start | bytes 393220
  11.5 64.5 %copy-start.1 = (bf16[1,512,128]{2,1,0:T(8,128)(2,1)S(1)}, bf16[1,512,128]{2,1,0:T(8,128)(2,1)}, u32[]{:S(2)}) copy-start(bf16[1,512,128]{2,1,0:T(8,128)(2,1)} %param.14) | copy-start | bytes 393220
  74.5 1.8 copy-start.2
  75.7 140.6 %reduce-scatter.3.cloned.1.call-start = ((), (), s32[]{:S(2)}) async-start(), calls=%async_computation.3 | async-start | bytes 8650752 | tf_op jit(solution)/shard_map/reduce_scatter | solution.py:130
  76.0 32.4 %copy-start.5 = (pred[512,512]{1,0:T(8,128)(4,1)}, pred[512,512]{1,0:T(8,128)(4,1)S(1)}, u32[]{:S(2)}) copy-start(pred[512,512]{1,0:T(8,128)(4,1)S(1)} %iota_compare_fusion) | copy-start | bytes 786436
  87.8 168.0 %reduce-scatter.5.cloned.1.call-start = ((), (), s32[]{:S(2)}) async-start(), calls=%async_computation.4 | async-start | bytes 294912 | tf_op jit(solution)/shard_map/reduce_scatter | solution.py:131
  114.4 3.5 %copy-start.7 = (s32[1,512,2]{1,2,0:T(2,128)S(1)}, s32[1,512,2]{1,2,0:T(2,128)}, u32[]{:S(2)}) copy-start(s32[1,512,2]{1,2,0:T(2,128)} %param.15) | copy-start | bytes 12292
  114.5 3.7 %copy-start.6 = (f32[512,1,128]{2,1,0:T(1,128)S(1)}, f32[512,1,128]{2,1,0:T(1,128)}, u32[]{:S(2)}) copy-start(f32[512,1,128]{2,1,0:T(1,128)} %fusion.45) | copy-start | bytes 786436
  115.5 100.8 %copy-start.3 = (f32[512,2,128]{0,2,1:T(8,128)S(1)}, f32[512,2,128]{0,2,1:T(8,128)}, u32[]{:S(2)}) copy-start(f32[512,2,128]{0,2,1:T(8,128)} %fusion.11) | copy-start | bytes 1572868
Sparse Core Ops, SparseCore 0:
  9.8 57.7 all-gather.4
  75.8 37.3 all-gather.6
  117.2 99.0 reduce-scatter.2
  219.4 36.4 reduce-scatter.4
where the time goes:
time: 263 us; the launch traced here: 262 us
  waiting for transfers between devices  114 us (43%)
  blocking collectives  89.9 us (34%)
  matrix products  33.1 us (13%)
  between operations  14 us (5%)
  other arithmetic  5.93 us (2%)
  local copies, waits for them, and re-layouts  4.61 us (2%)
    psum x1, blocking collectives, local(): rate_sum = lax.psum(rate_terms, ('dp', 'ctx'))  75.2 us
    all_gather x1, waiting for transfers between devices, local(): lax.all_gather(out_weight, 'ctx', axis=1, tiled=True)  56.1 us
    reduce_scatter x1, waiting for transfers between devices, local(): lax.psum_scatter(data_part, 'ctx', scatter_dimension=0, tiled=True)  36.1 us
    reduce_scatter x1, waiting for transfers between devices, local(): lax.psum_scatter(local_weight, 'dp', scatter_dimension=1, tiled=True)  21.4 us
    all_gather x1, blocking collectives, carried_in(): pieces = jax.tree.map(lambda part: lax.all_gather(part, axis), value)  14.7 us
    dot_general x1, matrix products, local(): lax.dot_general(outputs, grad_out, (((0,), (0,)), ((), ())), preferred_el...  9.06 us
    dot_general x1, matrix products, local(): lax.dot_general(grad_out, lax.all_gather(out_weight, 'ctx', axis=1, tiled...  6.93 us
  transfers between devices with their start and end apart: 4, of which 4 were waited for; matrix products, arithmetic and copies ran while one was open for 14% of the time, Pallas kernels for 0%

commit v1 on v0

--- a/solution.py
+++ b/solution.py
@@ -133,7 +133,7 @@
         inputs_local, inject_local, read_local, output_grad, log_decay, state_local, incoming
     )
     tokens_all = length * lax.axis_size("dp") * lax.axis_size("ctx")
-    rate_sum = lax.psum(rate_terms, ("dp", "ctx"))
+    rate_sum = jnp.sum(lax.all_gather(rate_terms, ("dp", "ctx")), axis=0)
     return (
         grad_input[None],
         grad_inject[None],

time: 263 us -> 303 us (1.15)
  waiting for transfers between devices: 114 us -> 153 us
    psum x1 -> x0, blocking collectives: 75.2 us -> none  [local(): rate_sum = lax.psum(rate_terms, ('dp', 'ctx'))]
    reduce_scatter x1, waiting for transfers between devices: 21.4 us -> 96.2 us  [local(): lax.psum_scatter(local_weight, 'dp', scatter_dimension=1, tiled=True)]
    unnamed x0 -> x1, blocking collectives: none -> 73.7 us
    reduce_scatter x1, waiting for transfers between devices: 36.1 us -> 0.01 us  [local(): lax.psum_scatter(data_part, 'ctx', scatter_dimension=0, tiled=True)]
  transfers between devices with their start and end apart: 4 -> 4, of which waited for: 4 -> 2; matrix products, arithmetic and copies ran while one was open for 14% -> 12% of each run, Pallas kernels for 0% -> 0%
where the time goes in v1:
time: 303 us; the launch traced here: 300 us
  waiting for transfers between devices  153 us (50%)
  blocking collectives  88.4 us (29%)
  matrix products  33.3 us (11%)
  between operations  14 us (5%)
  other arithmetic  5.98 us (2%)
  local copies, waits for them, and re-layouts  4.99 us (2%)
    reduce_scatter x1, waiting for transfers between devices, local(): lax.psum_scatter(local_weight, 'dp', scatter_dimension=1, tiled=True)  96.2 us
    unnamed x1, blocking collectives  73.7 us
    all_gather x1, waiting for transfers between devices, local(): lax.all_gather(out_weight, 'ctx', axis=1, tiled=True)  56.1 us
    all_gather x1, blocking collectives, carried_in(): pieces = jax.tree.map(lambda part: lax.all_gather(part, axis), value)  14.7 us
    dot_general x1, matrix products, local(): lax.dot_general(outputs, grad_out, (((0,), (0,)), ((), ())), preferred_el...  8.95 us
    dot_general x1, matrix products, local(): lax.dot_general(grad_out, lax.all_gather(out_weight, 'ctx', axis=1, tiled...  6.93 us
  transfers between devices with their start and end apart: 4, of which 2 were waited for; matrix products, arithmetic and copies ran while one was open for 12% of the time, Pallas kernels for 0%

profile of v1, /device:TPU:2, one launch (start us, length us, event | category | flops | bytes accessed | tf_op | source)
XLA Modules:
  0.0 300.1 jit_solution(7296443439108496380)
XLA Ops:
  7.2 0.7 all-gather.6.cloned.1.call-update
  7.9 0.7 neg.4
  8.6 0.8 fusion.61
  9.4 0.6 reduce-window.14
  10.0 0.2 slice_reduce_fusion.1
  10.1 0.2 reduce-window.15
  10.3 0.9 bitcast_convert_fusion.1
  11.3 0.1 copy.52
  11.5 56.1 %all-gather.6.cloned.1.call-done = bf16[256,8192]{1,0:T(8,128)(2,1)} async-done(((bf16[256,1024]{1,0:T(8,128)(2,1)}), bf16[256,8192]{1,0:T(8,128)(2,1)}) %all-gather.6.cloned.1.call-update) | async-done | bytes 4194320 | tf_op jit(solution)/shard_map/all_gather | solution.py:118
  67.6 6.9 %fusion.26 = bf16[512,256]{0,1:T(8,128)(2,1)S(1)} fusion(bf16[256,8192]{1,0:T(8,128)(2,1)} %all-gather.6.cloned.1.call-done, bf16[1,512,8192]{2,1,0:T(8,128)(2,1)} %param.10), kind=kOutput, calls=%fused_computation.24 | convolution fusion | flops 2147614720 | bytes 12845056 | tf_op jit(solution)/shard_map/dot_general | solution.py:116
  74.6 1.1 fusion.43
  75.7 0.1 copy.91
  76.0 0.3 fusion.55
  76.3 0.4 multiply_reduce_fusion.2
  76.8 2.0 fusion.22
  78.7 9.0 %fusion.1 = f32[256,8192]{1,0:T(8,128)} fusion(bf16[512,256]{0,1:T(8,128)(2,1)S(1)} %bitcast.164, bf16[1,512,8192]{2,1,0:T(8,128)(2,1)} %param.10), kind=kOutput, calls=%fused_computation.3 | convolution fusion | flops 2147483648 | bytes 17039360 | tf_op jit(solution)/shard_map/dot_general | solution.py:127
  87.8 0.2 slice_reduce_fusion.3
  88.0 14.7 %all-gather.2 = f32[8,1,2]{2,1,0:T(1,128)S(1)} all-gather(f32[1,1,2]{2,1,0:T(1,128)S(1)} %bitcast.175), channel_id=1, replica_groups=mesh['dp'=32,'ctx'=8] {'ctx'}, dimensions={0}, use_global_device_ids=true | all-gather | bytes 72 | tf_op jit(solution)/shard_map/all_gather | solution.py:11
  102.8 0.1 rev.14
  103.0 0.1 copy.72
  103.1 0.1 copy.89
  103.3 0.2 slice_reduce_fusion.2
  103.5 0.4 convolution_bitcast_fusion
  103.9 3.7 %fusion.45 = f32[512,1,128]{2,1,0:T(1,128)S(1)} fusion(f32[512,2,1]{1,2,0:T(1,128)S(1)} %copy.72, f32[512,2,128]{2,0,1:T(8,128)S(1)} %convolution_bitcast_fusion), kind=kOutput, calls=%fused_computation.47 | convolution fusion | flops 1572864 | bytes 790528 | tf_op jit(solution)/shard_map/th,thn->tn/dot_general | solution.py:81
  107.6 2.2 multiply_reduce_fusion
  109.8 1.3 fusion.29
  111.2 2.4 fusion.11
  113.5 1.3 rev.13
  114.8 0.9 while.14
  115.1 0.1 fusion.81
  115.8 0.1 fusion.49
  115.9 0.4 fusion.41
  116.3 0.2 multiply_reduce_fusion.4
  116.6 0.4 rev.15
  117.0 0.6 reduce-window.16
  117.6 0.2 slice_reduce_fusion
  117.7 0.2 reduce-window.19
  118.0 1.4 fusion.25
  119.4 96.2 %reduce-scatter.3.cloned.1.call-done = f32[256,256]{1,0:T(8,128)} async-done(((f32[256,8192]{1,0:T(8,128)}), f32[256,256]{1,0:T(8,128)}) %reduce-scatter.3.cloned.1.call-update) | async-done | bytes 262160 | tf_op jit(solution)/shard_map/reduce_scatter | solution.py:130
  215.7 0.1 copy.70
  215.9 0.8 copy.62
  216.7 0.4 rev.16
  217.1 0.2 multiply_reduce_fusion.3
  217.3 0.2 dynamic-update-slice
  217.5 73.7 %all-reduce = f32[512]{0:T(512)S(1)} all-reduce(f32[512]{0:T(512)S(1)} %dynamic-update-slice), channel_id=3, replica_groups=mesh['dp'=32,'ctx'=8] {'dp','ctx'}, use_global_device_ids=true, to_apply=%add | all-reduce | flops 512 | bytes 4096
  291.2 0.1 reshape.100
  291.4 1.7 fusion.30
  293.1 0.5 broadcast_multiply_fusion
  (54 shorter events, 1.5 us)
Async XLA Ops:
  7.2 60.4 %all-gather.6.cloned.1.call-start = ((), (), s32[]{:S(2)}) async-start(), calls=%async_computation.2 | async-start | bytes 4718592 | tf_op jit(solution)/shard_map/all_gather | solution.py:118
  7.9 105.6 %all-gather.8.cloned.1.call-start = ((), (), s32[]{:S(2)}) async-start(), calls=%async_computation.5 | async-start | bytes 1179648 | tf_op jit(solution)/shard_map/all_gather | solution.py:11
  11.5 64.2 %copy-start.3 = (bf16[1,512,256]{2,1,0:T(8,128)(2,1)S(1)}, bf16[1,512,256]{2,1,0:T(8,128)(2,1)}, u32[]{:S(2)}) copy-start(bf16[1,512,256]{2,1,0:T(8,128)(2,1)} %param.12) | copy-start | bytes 786436
  11.5 64.5 %copy-start = (bf16[1,512,128]{2,1,0:T(8,128)(2,1)S(1)}, bf16[1,512,128]{2,1,0:T(8,128)(2,1)}, u32[]{:S(2)}) copy-start(bf16[1,512,128]{2,1,0:T(8,128)(2,1)} %param.13) | copy-start | bytes 393220
  11.5 64.5 %copy-start.1 = (bf16[1,512,128]{2,1,0:T(8,128)(2,1)S(1)}, bf16[1,512,128]{2,1,0:T(8,128)(2,1)}, u32[]{:S(2)}) copy-start(bf16[1,512,128]{2,1,0:T(8,128)(2,1)} %param.14) | copy-start | bytes 393220
  74.5 1.8 copy-start.2
  75.7 140.0 %reduce-scatter.3.cloned.1.call-start = ((), (), s32[]{:S(2)}) async-start(), calls=%async_computation.3 | async-start | bytes 8650752 | tf_op jit(solution)/shard_map/reduce_scatter | solution.py:130
  76.0 2.7 copy-start.4
  87.7 205.9 %reduce-scatter.5.cloned.1.call-start = ((), (), s32[]{:S(2)}) async-start(), calls=%async_computation.4 | async-start | bytes 294912 | tf_op jit(solution)/shard_map/reduce_scatter | solution.py:131
  107.6 3.6 %copy-start.5 = (pred[512,512]{1,0:T(8,128)(4,1)S(1)}, pred[512,512]{1,0:T(8,128)(4,1)}, u32[]{:S(2)}) copy-start(pred[512,512]{1,0:T(8,128)(4,1)} %copy-done.4) | copy-start | bytes 786436
  115.9 101.2 %copy-start.6 = (s32[1,512,2]{1,2,0:T(2,128)S(1)}, s32[1,512,2]{1,2,0:T(2,128)}, u32[]{:S(2)}) copy-start(s32[1,512,2]{1,2,0:T(2,128)} %param.15) | copy-start | bytes 12292
Sparse Core Ops, SparseCore 0:
  9.8 57.7 all-gather.5
  75.8 37.3 all-gather.7
  117.1 98.4 reduce-scatter.2
  218.7 36.4 reduce-scatter.4
